TPU v7x, 256 devices: a whole 4x4x8 slice. The times are simulated.
256 devices in a mesh: tm: 16 (over x, y), space: 16 (over z, core).
Axes of the slice: x: 4, y: 4, z: 8, core: 2. Of those that a mesh axis runs over, the one named last changes fastest.
Arguments:
- clip: bfloat16 [256, 512, 768], P('tm', 'space'), may hold values from -160 to 160
- w_spatial: bfloat16 [4, 768, 768], replicated, may hold values from -4 to 4
- w_temporal: bfloat16 [4, 768, 768], replicated, may hold values from -4 to 4
Outputs:
- result: bfloat16 [256, 512, 768], P('tm', 'space')
All inputs are finite; a program needn't handle non-finite values.
Results may differ from a plain program's by a relative error of at most 0.011.
Values may be sent and summed in bfloat16 or wider, within the bound.
A program may use at most 128 MiB of HBM per device.

v0:
```python
import math
import jax
import jax.numpy as jnp
from jax import lax
from jax.sharding import PartitionSpec as P

HEAD = 64


def rms_norm(values):
    wide = values.astype(jnp.float32)
    return (wide * lax.rsqrt(jnp.mean(wide * wide, axis=-1, keepdims=True) + 1e-06)).astype(
        jnp.bfloat16
    )


def project_three(normed, weights):
    width = normed.shape[-1]
    flat = normed.reshape(-1, width)
    stacked = jnp.einsum(
        "rd,jde->jre", flat, weights[:3], preferred_element_type=jnp.float32
    ).astype(jnp.bfloat16)
    return (
        stacked[0].reshape(normed.shape),
        stacked[1].reshape(normed.shape),
        stacked[2].reshape(normed.shape),
    )


def out_project(mixed, weight):
    width = mixed.shape[-1]
    return jnp.dot(mixed.reshape(-1, width), weight, preferred_element_type=jnp.float32).reshape(
        mixed.shape
    )


def attend_frame(parts):
    query, key, value = parts
    count, width = query.shape
    heads = width // HEAD
    qh = query.reshape(count, heads, HEAD)
    kh = key.reshape(count, heads, HEAD)
    vh = value.reshape(count, heads, HEAD)
    scores = jnp.einsum("qhd,khd->hqk", qh, kh, preferred_element_type=jnp.float32) * (
        1.0 / math.sqrt(HEAD)
    )
    largest = jnp.max(scores, axis=-1, keepdims=True)
    expo = jnp.exp(scores - largest)
    weights = (expo / jnp.sum(expo, axis=-1, keepdims=True)).astype(jnp.bfloat16)
    mixed = jnp.einsum("hqk,khd->qhd", weights, vh, preferred_element_type=jnp.float32)
    return mixed.astype(jnp.bfloat16).reshape(count, width)


def frame_block(parts):
    inner = (parts[0][0], parts[1][0], parts[2][0])
    return lax.map(attend_frame, inner)[None]


def on_device(clip, w_spatial, w_temporal):
    frames, toks, width = clip.shape
    heads = width // HEAD
    space_count = lax.axis_size("space")
    frame_shape = (space_count, frames // space_count, toks, width)
    normed = rms_norm(clip)
    sq, sk, sv = project_three(normed, w_spatial)
    smix = frame_block(
        (
            lax.all_to_all(
                sq.reshape(frame_shape), "space", split_axis=0, concat_axis=2, tiled=True
            ),
            lax.all_to_all(
                sk.reshape(frame_shape), "space", split_axis=0, concat_axis=2, tiled=True
            ),
            lax.all_to_all(
                sv.reshape(frame_shape), "space", split_axis=0, concat_axis=2, tiled=True
            ),
        )
    )
    smix = lax.all_to_all(smix, "space", split_axis=2, concat_axis=0, tiled=True).reshape(
        frames, toks, width
    )
    after_space = (clip.astype(jnp.float32) + out_project(smix, w_spatial[3])).astype(jnp.bfloat16)
    tnormed = rms_norm(after_space)
    tq, tk, tv = project_three(tnormed, w_temporal)
    first_frame = lax.axis_index("tm") * frames
    qh = tq.reshape(frames, toks, heads, HEAD)
    query_pos = first_frame + jnp.arange(frames, dtype=jnp.int32)
    running = jnp.full((frames, toks, heads), -1e30, jnp.float32)
    key_piece = lax.all_gather(tk, "tm", axis=0, tiled=True)
    value_piece = lax.all_gather(tv, "tm", axis=0, tiled=True)
    count = key_piece.shape[0]
    kh = key_piece.reshape(count, toks, heads, HEAD)
    vh = value_piece.reshape(count, toks, heads, HEAD)
    scores = jnp.einsum("fphd,gphd->fphg", qh, kh, preferred_element_type=jnp.float32) * (
        1.0 / math.sqrt(HEAD)
    )
    key_pos = jnp.arange(count, dtype=jnp.int32)
    allowed = (key_pos[None, :] <= query_pos[:, None])[:, None, None, :]
    scores = jnp.where(allowed, scores, -1e30)
    newmax = jnp.maximum(running, jnp.max(scores, axis=-1))
    expo = jnp.where(allowed, jnp.exp(scores - newmax[..., None]), 0.0)
    total = jnp.sum(expo, axis=-1)
    acc = jnp.einsum("fphg,gphd->fphd", expo, vh.astype(jnp.float32))
    running, total, acc = (newmax, total, acc)
    tmix = (acc / total[..., None]).reshape(frames, toks, width).astype(jnp.bfloat16)
    return (after_space.astype(jnp.float32) + out_project(tmix, w_temporal[3])).astype(jnp.bfloat16)


def solution(mesh):
    placed = (P("tm", "space", None), P(), P())
    return jax.shard_map(
        on_device, mesh=mesh, in_specs=placed, out_specs=P("tm", "space", None), check_vma=False
    )
```

profile of v0, /device:TPU:1, one launch (start us, length us, event | category | flops | bytes accessed | tf_op | source)
XLA Modules:
  0.0 389.2 jit_solution(14649983245477244457)
XLA Ops:
  9.2 4.0 %convert_bitcast_fusion.1 = bf16[3,512,768]{2,1,0:T(8,128)(2,1)S(1)} fusion(bf16[512,768,1]{1,0,2:T(8,128)(2,1)S(1)} %bitcast.74, bf16[4,768,768]{2,1,0:T(8,128)(2,1)} %param.4), kind=kOutput, calls=%fused_computation.30 | convolution fusion | flops 1813118976 | bytes 6684672 | tf_op jit(solution)/shard_map/rd,jde->jre/dot_general | solution.py:20
  14.3 32.7 %all_to_all.16 = bf16[16,1,32,768]{3,2,1,0:T(8,128)(2,1)} all-to-all(bf16[16,1,32,768]{3,2,1,0:T(8,128)(2,1)S(1)} %bitcast.73), channel_id=1, replica_groups=mesh['tm'=16,'space'=16] {'space'}, dimensions={0} | all-to-all | bytes 1572864 | tf_op jit(solution)/shard_map/all_to_all | solution.py:68
  47.0 25.7 %all_to_all.17 = bf16[16,1,32,768]{3,2,1,0:T(8,128)(2,1)} all-to-all(bf16[16,1,32,768]{3,2,1,0:T(8,128)(2,1)S(1)} %bitcast.72), channel_id=1, replica_groups=mesh['tm'=16,'space'=16] {'space'}, dimensions={0} | all-to-all | bytes 1572864 | tf_op jit(solution)/shard_map/all_to_all | solution.py:71
  72.7 3.5 all-to-all-start
  76.4 2.7 reshape.105
  79.1 3.8 reshape.106
  82.9 8.0 %fusion.32 = f32[12,512,512]{1,2,0:T(8,128)} fusion(bf16[512,12,64]{2,1,0:T(8,128)(2,1)} %reshape.106, bf16[512,12,64]{2,1,0:T(8,128)(2,1)S(1)} %reshape.105), kind=kOutput, calls=%fused_computation.40 | convolution fusion | flops 402653184 | bytes 14155776 | tf_op jit(solution)/shard_map/while/body/eval_jaxpr/qhd,khd->hqk/dot_general | solution.py:44
  90.9 11.1 %fusion.55 = f32[12,512]{1,0:T(8,128)S(1)} fusion(f32[12,512,512]{1,2,0:T(8,128)} %fusion.32), kind=kOutput, calls=%fused_computation.61 | output fusion | flops 12583423 | bytes 12607488 | tf_op jit(solution)/shard_map/while/body/eval_jaxpr/sub | solution.py:48
  103.4 12.5 %fusion.35 = bf16[12,64,512]{2,1,0:T(8,128)(2,1)S(1)} fusion(f32[12,512]{1,0:T(8,128)S(1)} %fusion.55, bf16[512,12,64]{2,1,0:T(8,128)(2,1)S(1)} %reshape.104, f32[12,512,512]{1,2,0:T(8,128)} %fusion.32), kind=kOutput, calls=%fused_computation.43 | convolution fusion | flops 418781696 | bytes 14180352 | tf_op jit(solution)/shard_map/while/body/eval_jaxpr/hqk,khd->qhd/dot_general | solution.py:50
  115.8 1.8 copy.40
  118.2 5.5 %reduce = bf16[512,768]{1,0:T(8,128)(2,1)S(1)} reduce(bf16[512,1,1,768]{3,2,1,0:T(2,128)(2,1)S(1)} %bitcast.68, bf16[]{:T(256)} %broadcast.73), dimensions={1,2}, to_apply=%bitcast.56.reduce_sub_computation | reduce | bytes 1572866
  123.9 29.7 %all_to_all.18 = bf16[16,2,12288]{2,1,0:T(2,128)(2,1)S(1)} all-to-all(bf16[16,2,12288]{2,1,0:T(2,128)(2,1)S(1)} %reshape.114), channel_id=1, replica_groups=mesh['tm'=16,'space'=16] {'space'}, dimensions={0} | all-to-all | bytes 1572864 | tf_op jit(solution)/shard_map/all_to_all | solution.py:79
  154.4 2.2 fusion.26
  157.5 4.0 %convert_bitcast_fusion = bf16[3,512,768]{2,1,0:T(8,128)(2,1)S(1)} fusion(bf16[512,768,1]{1,0,2:T(8,128)(2,1)S(1)} %bitcast.75, bf16[4,768,768]{2,1,0:T(8,128)(2,1)} %param.5), kind=kOutput, calls=%fused_computation.29 | convolution fusion | flops 1813118976 | bytes 6684672 | tf_op jit(solution)/shard_map/rd,jde->jre/dot_general | solution.py:20
  165.2 89.3 %all-gather.5.cloned.1.call-done = bf16[256,32,768]{2,1,0:T(8,128)(2,1)} async-done(((bf16[16,32,768]{2,1,0:T(8,128)(2,1)}), bf16[256,32,768]{2,1,0:T(8,128)(2,1)}) %all-gather.5.cloned.1.call-update) | async-done | bytes 12582928 | tf_op jit(solution)/shard_map/all_gather | solution.py:89
  254.5 16.7 %copy.42 = bf16[256,32,768]{0,2,1:T(8,128)(2,1)} copy(bf16[256,32,768]{2,1,0:T(8,128)(2,1)} %all-gather.5.cloned.1.call-done) | data formatting | bytes 25165824 | tf_op jit(solution)/shard_map/all_gather | solution.py:89
  271.1 6.0 %fusion.6 = (f32[16,32,12]{0,2,1:T(8,128)S(1)}, f32[32,12,256,16]{2,3,1,0:T(8,128)S(1)}) fusion(pred[16,256]{1,0:T(8,128)(4,1)S(1)} %iota_compare_fusion, bf16[256,32,12,64]{0,3,2,1:T(8,128)(2,1)} %bitcast.66, bf16[16,32,12,64]{3,2,1,0:T(8,128)(2,1)S(1)} %reshape_reshape_squeeze.15), kind=kOutput, calls=%fused_computation.9 | convolution fusion | flops 206039040 | bytes 19689472 | tf_op jit(solution)/shard_map/fphd,gphd->fphg/dot_general | solution.py:94
  277.2 2.7 copy-done
  279.9 2.1 fusion.7
  282.0 69.5 %all-gather.3.cloned.1.call-done = bf16[256,32,768]{2,1,0:T(8,128)(2,1)} async-done(((bf16[16,32,768]{2,1,0:T(8,128)(2,1)}), bf16[256,32,768]{2,1,0:T(8,128)(2,1)}) %all-gather.3.cloned.1.call-update) | async-done | bytes 12582928 | tf_op jit(solution)/shard_map/all_gather | solution.py:90
  351.5 16.7 %copy.41 = bf16[256,32,768]{0,2,1:T(8,128)(2,1)} copy(bf16[256,32,768]{2,1,0:T(8,128)(2,1)} %all-gather.3.cloned.1.call-done) | data formatting | bytes 25165824 | tf_op jit(solution)/shard_map/all_gather | solution.py:90
  368.3 8.3 %fusion.13 = bf16[16,32,12,64]{3,0,2,1:T(8,128)(2,1)S(1)} fusion(f32[16,32,12]{0,2,1:T(8,128)S(1)} %fusion.7, bf16[256,32,12,64]{0,3,2,1:T(8,128)(2,1)} %bitcast.67, f32[32,12,256,16]{2,3,1,0:T(8,128)} %copy-done, f32[16,32,12]{0,2,1:T(8,128)S(1)} %broadcast_maximum_fusion, pred[16,256]{1,0:T(8,128)(4,1)S(1)} %iota_compare_fusion), kind=kOutput, calls=%fused_computation.17 | convolution fusion | flops 208404480 | bytes 19714048 | tf_op jit(solution)/shard_map/fphg,gphd->fphd/dot_general | solution.py:103
  377.1 2.0 convert_element_type.65
  379.2 3.2 fusion.28
  (29 shorter events, 11.9 us)
Async XLA Ops:
  72.7 29.4 %all-to-all-start = ((bf16[16,1,32,768]{3,2,1,0:T(8,128)(2,1)}), bf16[16,1,32,768]{3,2,1,0:T(8,128)(2,1)S(1)}, u32[]{:S(2)}, u32[]{:S(2)}) async-start(bf16[16,1,32,768]{3,2,1,0:T(8,128)(2,1)} %bitcast.4), calls=%async_computation | async-start | bytes 1572864 | tf_op jit(solution)/shard_map/all_to_all | solution.py:74
  76.2 178.3 %all-gather.5.cloned.1.call-start = ((), (), s32[]{:S(2)}) async-start(), calls=%async_computation.5 | async-start | bytes 13369344 | tf_op jit(solution)/shard_map/all_gather | solution.py:89
  118.2 36.2 %copy-start.1 = (bf16[16,32,768]{2,1,0:T(8,128)(2,1)S(1)}, bf16[16,32,768]{2,1,0:T(8,128)(2,1)}, u32[]{:S(2)}) copy-start(bf16[16,32,768]{2,1,0:T(8,128)(2,1)} %param.3) | copy-start | bytes 2359300
  156.6 0.9 copy-start.2
  162.9 188.6 %all-gather.3.cloned.1.call-start = ((), (), s32[]{:S(2)}) async-start(), calls=%async_computation.4 | async-start | bytes 13369344 | tf_op jit(solution)/shard_map/all_gather | solution.py:90
  277.2 2.7 copy-start
  376.6 2.6 copy-start.3
Sparse Core Ops, SparseCore 0:
  163.0 91.4 all-gather.4
  256.9 94.5 all-gather.2
where the time goes:
time: 391 us; the launch traced here: 389 us
  waiting for transfers between devices  159 us (41%)
  blocking collectives  88 us (23%)
  local copies, waits for them, and re-layouts  54.3 us (14%)
  matrix products  48.2 us (12%)
  other arithmetic  21.7 us (6%)
  between operations  13.6 us (3%)
    all_gather x1, waiting for transfers between devices, on_device(): key_piece = lax.all_gather(tk, 'tm', axis=0, tiled=True)  89.3 us
    all_gather x1, waiting for transfers between devices, on_device(): value_piece = lax.all_gather(tv, 'tm', axis=0, tiled=True)  69.5 us
    all_to_all x1, blocking collectives, on_device(): lax.all_to_all(sq.reshape(frame_shape), 'space', split_axis=0, concat_axi...  32.7 us
    all_to_all x1, blocking collectives, on_device(): lax.all_to_all(smix, 'space', split_axis=2, concat_axis=0, tiled=True)  29.7 us
    all_to_all x1, blocking collectives, on_device(): lax.all_to_all(sk.reshape(frame_shape), 'space', split_axis=0, concat_axi...  25.7 us
    all_gather x1, local copies, waits for them, and re-layouts, on_device(): value_piece = lax.all_gather(tv, 'tm', axis=0, tiled=True)  16.7 us
    all_gather x1, local copies, waits for them, and re-layouts, on_device(): key_piece = lax.all_gather(tk, 'tm', axis=0, tiled=True)  16.7 us
    dot_general x1, matrix products, attend_frame(): jnp.einsum('hqk,khd->qhd', weights, vh, preferred_element_type=jnp.float32)  12.5 us
  transfers between devices with their start and end apart: 3, of which 2 were waited for; matrix products, arithmetic and copies ran while one was open for 13% of the time, Pallas kernels for 0%

commit v1 on v0

--- a/solution.py
+++ b/solution.py
@@ -86,8 +86,11 @@
     qh = tq.reshape(frames, toks, heads, HEAD)
     query_pos = first_frame + jnp.arange(frames, dtype=jnp.int32)
     running = jnp.full((frames, toks, heads), -1e30, jnp.float32)
-    key_piece = lax.all_gather(tk, "tm", axis=0, tiled=True)
-    value_piece = lax.all_gather(tv, "tm", axis=0, tiled=True)
+    key_piece, value_piece = jnp.split(
+        lax.all_gather(jnp.concatenate([tk, tv], axis=1), "tm", axis=0, tiled=True),
+        [tk.shape[1]],
+        axis=1,
+    )
     count = key_piece.shape[0]
     kh = key_piece.reshape(count, toks, heads, HEAD)
     vh = value_piece.reshape(count, toks, heads, HEAD)

time: 391 us -> 405 us (1.036)
  local copies, waits for them, and re-layouts: 54.3 us -> 68 us
    split x0 -> x3, local copies, waits for them, and re-layouts: none -> 51.2 us  [on_device(): jnp.split(lax.all_gather(jnp.concatenate([tk, tv], axis=1), 'tm', axis=0,...]
    all_gather x2 -> x0, local copies, waits for them, and re-layouts: 33.4 us -> none  [the longest x1 16.7 us: on_device(): value_piece = lax.all_gather(tv, 'tm', axis=0, tiled=True)]
    all_gather x2 -> x1, waiting for transfers between devices: 159 us -> 155 us  [on_device(): lax.all_gather(jnp.concatenate([tk, tv], axis=1), 'tm', axis=0, tiled=True)]
  transfers between devices with their start and end apart: 3 -> 2, of which waited for: 2 -> 1; matrix products, arithmetic and copies ran while one was open for 13% -> 7% of each run, Pallas kernels for 0% -> 0%
where the time goes in v1:
time: 405 us; the launch traced here: 404 us
  waiting for transfers between devices  155 us (38%)
  blocking collectives  88 us (22%)
  local copies, waits for them, and re-layouts  68 us (17%)
  matrix products  50.3 us (12%)
  other arithmetic  25.6 us (6%)
  between operations  13.6 us (3%)
    all_gather x1, waiting for transfers between devices, on_device(): lax.all_gather(jnp.concatenate([tk, tv], axis=1), 'tm', axis=0, tiled=True)  155 us
    split x3, local copies, waits for them, and re-layouts, on_device(): jnp.split(lax.all_gather(jnp.concatenate([tk, tv], axis=1), 'tm', axis=0,...  51.2 us
    all_to_all x1, blocking collectives, on_device(): lax.all_to_all(sq.reshape(frame_shape), 'space', split_axis=0, concat_axi...  32.7 us
    all_to_all x1, blocking collectives, on_device(): lax.all_to_all(smix, 'space', split_axis=2, concat_axis=0, tiled=True)  29.7 us
    all_to_all x1, blocking collectives, on_device(): lax.all_to_all(sk.reshape(frame_shape), 'space', split_axis=0, concat_axi...  25.7 us
    dot_general x1, matrix products, attend_frame(): jnp.einsum('hqk,khd->qhd', weights, vh, preferred_element_type=jnp.float32)  12.5 us
    sub x1, other arithmetic, attend_frame(): expo = jnp.exp(scores - largest)  11.1 us
    dot_general x1, matrix products, on_device(): jnp.einsum('fphd,gphd->fphg', qh, kh, preferred_element_type=jnp.float32)  9.83 us
  transfers between devices with their start and end apart: 2, of which 1 were waited for; matrix products, arithmetic and copies ran while one was open for 7% of the time, Pallas kernels for 0%

profile of v1, /device:TPU:1, one launch (start us, length us, event | category | flops | bytes accessed | tf_op | source)
XLA Modules:
  0.0 403.9 jit_solution(5573602639482686183)
XLA Ops:
  6.5 1.4 fusion.23
  9.2 4.0 convert_bitcast_fusion.1
  14.3 32.7 %all_to_all.16 = bf16[16,1,32,768]{3,2,1,0:T(8,128)(2,1)} all-to-all(bf16[16,1,32,768]{3,2,1,0:T(8,128)(2,1)S(1)} %bitcast.71), channel_id=1, replica_groups=mesh['tm'=16,'space'=16] {'space'}, dimensions={0} | all-to-all | bytes 1572864 | tf_op jit(solution)/shard_map/all_to_all | solution.py:68
  47.0 25.7 %all_to_all.17 = bf16[16,1,32,768]{3,2,1,0:T(8,128)(2,1)} all-to-all(bf16[16,1,32,768]{3,2,1,0:T(8,128)(2,1)S(1)} %bitcast.70), channel_id=1, replica_groups=mesh['tm'=16,'space'=16] {'space'}, dimensions={0} | all-to-all | bytes 1572864 | tf_op jit(solution)/shard_map/all_to_all | solution.py:71
  72.7 3.5 all-to-all-start
  76.4 2.7 reshape.105
  79.1 3.8 reshape.106
  82.9 8.0 %fusion.32 = f32[12,512,512]{1,2,0:T(8,128)} fusion(bf16[512,12,64]{2,1,0:T(8,128)(2,1)} %reshape.106, bf16[512,12,64]{2,1,0:T(8,128)(2,1)S(1)} %reshape.105), kind=kOutput, calls=%fused_computation.41 | convolution fusion | flops 402653184 | bytes 14155776 | tf_op jit(solution)/shard_map/while/body/eval_jaxpr/qhd,khd->hqk/dot_general | solution.py:44
  90.9 11.1 %fusion.56 = f32[12,512]{1,0:T(8,128)S(1)} fusion(f32[12,512,512]{1,2,0:T(8,128)} %fusion.32), kind=kOutput, calls=%fused_computation.63 | output fusion | flops 12583423 | bytes 12607488 | tf_op jit(solution)/shard_map/while/body/eval_jaxpr/sub | solution.py:48
  103.4 12.5 %fusion.35 = bf16[12,64,512]{2,1,0:T(8,128)(2,1)S(1)} fusion(f32[12,512]{1,0:T(8,128)S(1)} %fusion.56, bf16[512,12,64]{2,1,0:T(8,128)(2,1)S(1)} %reshape.104, f32[12,512,512]{1,2,0:T(8,128)} %fusion.32), kind=kOutput, calls=%fused_computation.44 | convolution fusion | flops 418781696 | bytes 14180352 | tf_op jit(solution)/shard_map/while/body/eval_jaxpr/hqk,khd->qhd/dot_general | solution.py:50
  115.8 1.8 copy.40
  118.2 5.5 %reduce = bf16[512,768]{1,0:T(8,128)(2,1)S(1)} reduce(bf16[512,1,1,768]{3,2,1,0:T(2,128)(2,1)S(1)} %bitcast.68, bf16[]{:T(256)} %broadcast.73), dimensions={1,2}, to_apply=%bitcast.56.reduce_sub_computation | reduce | bytes 1572866
  123.9 29.7 %all_to_all.18 = bf16[16,2,12288]{2,1,0:T(2,128)(2,1)S(1)} all-to-all(bf16[16,2,12288]{2,1,0:T(2,128)(2,1)S(1)} %reshape.114), channel_id=1, replica_groups=mesh['tm'=16,'space'=16] {'space'}, dimensions={0} | all-to-all | bytes 1572864 | tf_op jit(solution)/shard_map/all_to_all | solution.py:79
  154.4 2.2 fusion.26
  157.5 4.0 convert_bitcast_fusion
  164.4 154.5 %all-gather.2.cloned.1.call-done = bf16[256,64,768]{2,1,0:T(8,128)(2,1)} async-done(((bf16[16,64,768]{2,1,0:T(8,128)(2,1)}), bf16[256,64,768]{2,1,0:T(8,128)(2,1)}) %all-gather.2.cloned.1.call-update) | async-done | bytes 25165840 | tf_op jit(solution)/shard_map/all_gather | solution.py:90
  318.9 17.7 %fusion.53 = (bf16[256,32,768]{2,1,0:T(8,128)(2,1)}, bf16[256,32,768]{2,1,0:T(8,128)(2,1)}) fusion(bf16[256,64,768]{2,1,0:T(8,128)(2,1)} %all-gather.2.cloned.1.call-done), kind=kLoop, calls=%fused_computation.60 | loop fusion | bytes 50331648 | tf_op jit(solution)/shard_map/split | solution.py:89
  336.6 16.7 %copy.42 = bf16[256,32,768]{0,2,1:T(8,128)(2,1)} copy(bf16[256,32,768]{2,1,0:T(8,128)(2,1)} %get-tuple-element.14) | data formatting | bytes 25165824 | tf_op jit(solution)/shard_map/split | solution.py:89
  353.4 9.8 %fusion.6 = (f32[16,32,12]{0,2,1:T(8,128)S(1)}, f32[32,12,256,16]{2,3,1,0:T(8,128)}) fusion(pred[16,256]{1,0:T(8,128)(4,1)S(1)} %iota_compare_fusion, bf16[256,32,12,64]{0,3,2,1:T(8,128)(2,1)} %bitcast.66, bf16[16,32,12,64]{3,2,1,0:T(8,128)(2,1)S(1)} %reshape_reshape_squeeze.15), kind=kOutput, calls=%fused_computation.9 | convolution fusion | flops 206039040 | bytes 19689472 | tf_op jit(solution)/shard_map/fphd,gphd->fphg/dot_general | solution.py:97
  363.2 16.7 %copy.41 = bf16[256,32,768]{0,2,1:T(8,128)(2,1)} copy(bf16[256,32,768]{2,1,0:T(8,128)(2,1)} %get-tuple-element.13) | data formatting | bytes 25165824 | tf_op jit(solution)/shard_map/split | solution.py:89
  380.0 4.7 %fusion.7 = f32[16,32,12]{0,2,1:T(8,128)S(1)} fusion(f32[32,12,256,16]{2,3,1,0:T(8,128)} %get-tuple-element.31, f32[16,32,12]{0,2,1:T(8,128)S(1)} %broadcast_maximum_fusion, pred[16,256]{1,0:T(8,128)(4,1)S(1)} %iota_compare_fusion), kind=kLoop, calls=%fused_computation.10 | loop fusion | flops 7858176 | bytes 6344704 | tf_op jit(solution)/shard_map/reduce_sum | solution.py:105
  384.6 6.7 %fusion.13 = bf16[16,32,12,64]{3,0,2,1:T(8,128)(2,1)S(1)} fusion(f32[16,32,12]{0,2,1:T(8,128)S(1)} %fusion.7, bf16[256,32,12,64]{0,3,2,1:T(8,128)(2,1)} %bitcast.67, f32[32,12,256,16]{2,3,1,0:T(8,128)S(1)} %copy-done, f32[16,32,12]{0,2,1:T(8,128)S(1)} %broadcast_maximum_fusion, pred[16,256]{1,0:T(8,128)(4,1)S(1)} %iota_compare_fusion), kind=kOutput, calls=%fused_computation.17 | convolution fusion | flops 208404480 | bytes 19714048 | tf_op jit(solution)/shard_map/fphg,gphd->fphd/dot_general | solution.py:106
  391.9 2.0 convert_element_type.65
  393.9 3.2 fusion.28
  (28 shorter events, 9.7 us)
Async XLA Ops:
  72.7 29.4 %all-to-all-start = ((bf16[16,1,32,768]{3,2,1,0:T(8,128)(2,1)}), bf16[16,1,32,768]{3,2,1,0:T(8,128)(2,1)S(1)}, u32[]{:S(2)}, u32[]{:S(2)}) async-start(bf16[16,1,32,768]{3,2,1,0:T(8,128)(2,1)} %bitcast.4), calls=%async_computation | async-start | bytes 1572864 | tf_op jit(solution)/shard_map/all_to_all | solution.py:74
  76.2 242.7 %all-gather.2.cloned.1.call-start = ((), (), s32[]{:S(2)}) async-start(), calls=%async_computation.4 | async-start | bytes 26738688 | tf_op jit(solution)/shard_map/all_gather | solution.py:90
  118.2 36.2 %copy-start.1 = (bf16[16,32,768]{2,1,0:T(8,128)(2,1)S(1)}, bf16[16,32,768]{2,1,0:T(8,128)(2,1)}, u32[]{:S(2)}) copy-start(bf16[16,32,768]{2,1,0:T(8,128)(2,1)} %param.3) | copy-start | bytes 2359300
  156.6 0.9 copy-start.2
  380.0 4.7 %copy-start = (f32[32,12,256,16]{2,3,1,0:T(8,128)S(1)}, f32[32,12,256,16]{2,3,1,0:T(8,128)}, u32[]{:S(2)}) copy-start(f32[32,12,256,16]{2,3,1,0:T(8,128)} %get-tuple-element.31) | copy-start | bytes 18874372
  391.3 2.6 copy-start.3
Sparse Core Ops, SparseCore 0:
  163.1 155.7 all-gather.1
